TPU v7x, 32 devices: a whole 2x2x4 slice. The times are simulated.
32 devices in a mesh: groups: 2 (over x), seq: 16 (over z, y, core).
Axes of the slice: x: 2, y: 2, z: 4, core: 2. Of those that a mesh axis runs over, the one named last changes fastest.
Arguments:
- hidden: bfloat16 [64, 16384], P('groups', 'seq'), parts along dimension 0, may hold values from -6 to 6
- w_query: bfloat16 [16384, 8192], P('seq'), may hold values from -0.046875 to 0.046875
- w_key: bfloat16 [16384, 512], P('seq'), may hold values from -0.25 to 0.25
- w_value: bfloat16 [16384, 512], P('seq'), may hold values from -0.1875 to 0.1875
- w_out: bfloat16 [8192, 16384], P(None, 'seq'), may hold values from -0.0625 to 0.0625
- prefix_keys: bfloat16 [65536, 512], P(('groups', 'seq')), parts along dimension 0, may hold values from -6 to 6
- prefix_values: bfloat16 [65536, 512], P(('groups', 'seq')), parts along dimension 0, may hold values from -6 to 6
- key_scales: float32 [512, 4], P(('groups', 'seq')), parts along dimension 0, may hold values from 1 to 2.5
- value_scales: float32 [512, 4], P(('groups', 'seq')), parts along dimension 0, may hold values from 0.5 to 2
- demo_keys: bfloat16 [32, 2048, 512], P('groups', 'seq'), parts along dimension 0, may hold values from -200 to 200
- demo_values: bfloat16 [32, 2048, 512], P('groups', 'seq'), parts along dimension 0, may hold values from -12 to 12
- task_ids: int32 [64], P('groups'), parts along dimension 0, may hold values from 0 to 15
- demo_lengths: int32 [32], P('groups'), parts along dimension 0, may hold values from 1 to 2048, 16384 in all
- offsets: int32 [64], P('groups'), parts along dimension 0, may hold values from 0 to 31
Outputs:
- mixed: bfloat16 [64, 16384], P('groups', 'seq'), parts along dimension 0
There are 2 independent parts, one for each index of `groups`. A program takes and returns all parts, laid end to end along the dimension named above; an argument that names none is the same for every part. Nothing has to cross between parts.
Inputs may be any that keep to these rules, and one draw needn't show every extreme that they name: `demo_lengths`: the largest is exactly 2048.
All inputs are finite; a program needn't handle non-finite values.
Results may differ from a plain program's by a relative error of at most 0.007.
The roundings to bfloat16 on the way count: a program that leaves them out, or rounds other values in their place, can miss the bound.
Values may be sent and summed in bfloat16 or wider, within the bound.
A program may use at most 128 MiB of HBM per device.

v0:
```python
import math

import jax
import jax.numpy as jnp
from jax import lax
from jax.sharding import PartitionSpec as P

HD = 128


NEG = -1e30


def head_part(args):
    q_rows, p_keys, p_vals, k_scale, v_scale, d_keys, d_vals, s_keys, s_vals, d_mask, s_mask = args
    inv = 1.0 / math.sqrt(HD)
    s_pre = jnp.dot(q_rows, p_keys.T, preferred_element_type=jnp.float32) * (k_scale[None, :] * inv)
    s_demo = jnp.where(
        d_mask, jnp.dot(q_rows, d_keys.T, preferred_element_type=jnp.float32) * inv, NEG
    )
    s_self = jnp.where(
        s_mask, jnp.dot(q_rows, s_keys.T, preferred_element_type=jnp.float32) * inv, NEG
    )
    top = jnp.maximum(
        jnp.maximum(jnp.max(s_pre, axis=1), jnp.max(s_demo, axis=1)), jnp.max(s_self, axis=1)
    )
    e_pre = jnp.exp(s_pre - top[:, None])
    e_demo = jnp.exp(s_demo - top[:, None])
    e_self = jnp.exp(s_self - top[:, None])
    total = jnp.sum(e_pre, axis=1) + jnp.sum(e_demo, axis=1) + jnp.sum(e_self, axis=1)
    acc = jnp.dot(
        (e_pre * v_scale[None, :]).astype(jnp.bfloat16), p_vals, preferred_element_type=jnp.float32
    )
    acc = acc + jnp.dot(e_demo.astype(jnp.bfloat16), d_vals, preferred_element_type=jnp.float32)
    acc = acc + jnp.dot(e_self.astype(jnp.bfloat16), s_vals, preferred_element_type=jnp.float32)
    return (top, total, acc)


def body(
    hidden,
    w_query,
    w_key,
    w_value,
    w_out,
    prefix_keys,
    prefix_values,
    key_scales,
    value_scales,
    demo_keys,
    demo_values,
    task_ids,
    demo_lengths,
    offsets,
):
    devices = lax.axis_size("seq")
    index = lax.axis_index("seq")
    qtok = hidden.shape[0]
    per_dev = qtok // devices
    kvh = prefix_keys.shape[1] // HD
    heads = w_query.shape[1] // HD
    group = heads // kvh
    part_q = jnp.dot(hidden, w_query, preferred_element_type=jnp.float32)
    part_k = jnp.dot(hidden, w_key, preferred_element_type=jnp.float32)
    part_v = jnp.dot(hidden, w_value, preferred_element_type=jnp.float32)
    query, s_keys, s_vals = lax.psum((part_q, part_k, part_v), "seq")
    query = query.astype(jnp.bfloat16)
    s_keys = s_keys.astype(jnp.bfloat16)
    s_vals = s_vals.astype(jnp.bfloat16)
    pre_dev = prefix_keys.shape[0]
    blocks = key_scales.shape[0]
    tasks = demo_keys.shape[0]
    demo_dev = demo_keys.shape[1]
    q_heads = (
        query.reshape(qtok, kvh, group, HD).transpose(1, 0, 2, 3).reshape(kvh, qtok * group, HD)
    )
    p_keys = prefix_keys.reshape(pre_dev, kvh, HD).transpose(1, 0, 2)
    p_vals = prefix_values.reshape(pre_dev, kvh, HD).transpose(1, 0, 2)
    k_scale = jnp.repeat(key_scales, pre_dev // blocks, axis=0).T
    v_scale = jnp.repeat(value_scales, pre_dev // blocks, axis=0).T
    d_keys = demo_keys.reshape(tasks * demo_dev, kvh, HD).transpose(1, 0, 2)
    d_vals = demo_values.reshape(tasks * demo_dev, kvh, HD).transpose(1, 0, 2)
    own_keys = lax.dynamic_slice_in_dim(s_keys, index * per_dev, per_dev, 0)
    own_vals = lax.dynamic_slice_in_dim(s_vals, index * per_dev, per_dev, 0)
    sk = own_keys.reshape(per_dev, kvh, HD).transpose(1, 0, 2)
    sv = own_vals.reshape(per_dev, kvh, HD).transpose(1, 0, 2)
    slot = jnp.arange(tasks * demo_dev, dtype=jnp.int32)
    demo_task = slot // demo_dev
    demo_pos = index * demo_dev + slot % demo_dev
    key_len = jnp.sum(
        jnp.where(
            demo_task[:, None] == jnp.arange(tasks, dtype=jnp.int32)[None, :],
            demo_lengths[None, :],
            0,
        ),
        axis=1,
    )
    d_mask = (task_ids[:, None] == demo_task[None, :]) & (demo_pos < key_len)[None, :]
    own_task = lax.dynamic_slice_in_dim(task_ids, index * per_dev, per_dev, 0)
    own_off = lax.dynamic_slice_in_dim(offsets, index * per_dev, per_dev, 0)
    s_mask = (task_ids[:, None] == own_task[None, :]) & (own_off[None, :] <= offsets[:, None])
    d_mask = jnp.repeat(d_mask, group, axis=0)
    s_mask = jnp.repeat(s_mask, group, axis=0)

    def run(h):
        return head_part(
            (
                q_heads[h],
                p_keys[h],
                p_vals[h],
                k_scale[h],
                v_scale[h],
                d_keys[h],
                d_vals[h],
                sk[h],
                sv[h],
                d_mask,
                s_mask,
            )
        )

    top, total, acc = lax.map(run, jnp.arange(kvh, dtype=jnp.int32))
    top = top.reshape(kvh, qtok, group).transpose(1, 0, 2).reshape(qtok, heads)
    total = total.reshape(kvh, qtok, group).transpose(1, 0, 2).reshape(qtok, heads)
    acc = acc.reshape(kvh, qtok, group, HD).transpose(1, 0, 2, 3).reshape(qtok, heads, HD)
    peak = lax.pmax(top, "seq")
    factor = jnp.exp(top - peak)
    own_total, own_acc = (
        lax.psum_scatter(total * factor, "seq", scatter_dimension=0, tiled=True),
        lax.psum_scatter(acc * factor[..., None], "seq", scatter_dimension=0, tiled=True),
    )
    own_rows = (own_acc / own_total[..., None]).astype(jnp.bfloat16).reshape(per_dev, heads * HD)
    attended = lax.all_gather(own_rows, "seq", axis=0, tiled=True)
    return jnp.dot(attended, w_out, preferred_element_type=jnp.float32).astype(jnp.bfloat16)


def solution(mesh):
    placed = (
        P("groups", "seq"),
        P("seq", None),
        P("seq", None),
        P("seq", None),
        P(None, "seq"),
        P(("groups", "seq"), None),
        P(("groups", "seq"), None),
        P(("groups", "seq"), None),
        P(("groups", "seq"), None),
        P("groups", "seq", None),
        P("groups", "seq", None),
        P("groups"),
        P("groups"),
        P("groups"),
    )
    return jax.shard_map(
        body, mesh=mesh, in_specs=placed, out_specs=P("groups", "seq"), check_vma=False
    )
```

profile of v0, /device:TPU:0, one launch (start us, length us, event | category | flops | bytes accessed | tf_op | source)
XLA Modules:
  0.0 325.1 jit_solution(12262820651837910911)
XLA Ops:
  6.6 0.8 dynamic_slice.45
  7.4 0.7 dynamic_slice.44
  8.1 0.8 broadcast_bitcast_fusion.1
  8.9 0.8 broadcast_bitcast_fusion
  9.6 0.8 select_reduce_fusion
  10.4 0.8 compare_and_fusion
  11.2 1.1 fusion.54
  12.3 1.6 fusion.55
  13.8 8.8 %fusion.53 = f32[32,8192]{1,0:T(8,128)S(1)} fusion(bf16[32,1024]{1,0:T(8,128)(2,1)} %param.16, bf16[1024,8192]{1,0:T(8,128)(2,1)} %param.17), kind=kOutput, calls=%fused_computation.86 | convolution fusion | flops 536870912 | bytes 17891328 | tf_op jit(solution)/shard_map/dot_general | solution.py:62
  22.6 75.0 %all-reduce.3 = (bf16[32,8192]{1,0:T(8,128)(2,1)S(1)}, bf16[32,512]{1,0:T(8,128)(2,1)S(1)}, bf16[32,512]{1,0:T(8,128)(2,1)S(1)}) all-reduce(f32[32,8192]{1,0:T(8,128)S(1)} %fusion.53, f32[32,512]{1,0:T(8,128)S(1)} %fusion.54, f32[32,512]{1,0:T(8,128)S(1)} %fusion.55), channel_id=1, replica_groups=mesh['groups'=2,'seq'=16] {'seq'}, use_global_device_ids=true, to_apply=%region_0.0 | all-reduce | flops 294912 | bytes 1769472 | tf_op jit(solution)/shard_map/psum | solution.py:65
  97.8 2.9 copy.58
  100.8 4.0 %copy.60 = bf16[2048,512]{0,1:T(8,128)(2,1)} copy(bf16[2048,512]{1,0:T(8,128)(2,1)} %param.22) | data formatting | bytes 4194304 | tf_op args[6]
  104.8 4.0 %reshape.181 = bf16[2048,4,128]{2,1,0:T(4,128)(2,1)} reshape(bf16[16,128,512]{2,1,0:T(8,128)(2,1)} %param.25) | data formatting | bytes 4194304 | tf_op jit(solution)/shard_map/reshape | solution.py:80
  108.8 4.0 %reshape.182 = bf16[2048,4,128]{2,1,0:T(4,128)(2,1)} reshape(bf16[16,128,512]{2,1,0:T(8,128)(2,1)} %param.26) | data formatting | bytes 4194304 | tf_op jit(solution)/shard_map/reshape | solution.py:81
  112.9 4.8 %copy_bitcast_fusion = (bf16[4,2048,128]{2,1,0:T(8,128)(2,1)}, bf16[4,2048,128]{2,1,0:T(8,128)(2,1)}) fusion(bf16[2048,4,128]{2,1,0:T(4,128)(2,1)} %reshape.182, bf16[2048,4,128]{2,1,0:T(4,128)(2,1)} %reshape.181), kind=kLoop, calls=%fused_computation.51 | loop fusion | bytes 8388608
  117.7 50.9 %while.15 = (s32[]{:T(128)}, f32[4,512]{1,0:T(4,128)S(1)}, f32[4,512]{1,0:T(4,128)S(1)}, f32[4,512,128]{2,1,0:T(8,128)}, s32[4]{0:T(128)S(1)}, /*index=5*/bf16[4...) while((s32[]{:T(128)}, f32[4,512]{1,0:T(4,128)S(1)}, ...), condition=%wide.region_11.12_spmd.clone, body=%wide.region_4.11_spmd.clone.sunk | while | flops 1092231168 | bytes 29230400 | solution.py:121
  117.7 0.6 dynamic_slice.136
  120.4 0.8 multiply_reduce_fusion.2
  121.2 2.0 fusion.82
  123.3 2.2 fusion.84
  125.5 2.0 fusion.85
  127.5 1.8 convolution_add_fusion.3
  129.5 1.0 fusion.86
  133.1 0.8 multiply_reduce_fusion.2
  133.9 2.0 fusion.82
  136.0 2.2 fusion.84
  138.2 2.0 fusion.85
  140.2 1.8 convolution_add_fusion.3
  142.2 1.0 fusion.86
  145.9 0.8 multiply_reduce_fusion.2
  146.7 2.0 fusion.82
  148.7 2.2 fusion.84
  150.9 2.0 fusion.85
  153.0 1.8 convolution_add_fusion.3
  154.9 1.0 fusion.86
  158.6 0.8 multiply_reduce_fusion.2
  159.4 2.0 fusion.82
  161.4 2.2 fusion.84
  163.7 2.0 fusion.85
  165.7 1.8 convolution_add_fusion.3
  167.6 1.0 fusion.86
  168.6 1.4 copy.66
  170.1 57.6 %pmax.7 = f32[32,64]{0,1:T(8,128)S(1)} all-reduce(f32[32,64]{0,1:T(8,128)S(1)} %bitcast.174), channel_id=1, replica_groups=mesh['groups'=2,'seq'=16] {'seq'}, use_global_device_ids=true, to_apply=%region_12.13 | all-reduce | flops 2048 | bytes 16384 | tf_op jit(solution)/shard_map/pmax | solution.py:125
  228.0 1.3 bitcast_multiply_fusion
  230.6 57.9 %all-reduce = f32[32,64]{0,1:T(8,128)S(1)} all-reduce(f32[32,64]{0,1:T(8,128)S(1)} %get-tuple-element.230), channel_id=3, replica_groups=mesh['groups'=2,'seq'=16] {'seq'}, use_global_device_ids=true, to_apply=%region_14.15.clone | all-reduce | flops 2048 | bytes 16384
  288.7 0.9 divide_convert_fusion
  289.6 18.9 %all-gather = bf16[16,2,8192]{2,1,0:T(2,128)(2,1)S(1)} all-gather(bf16[1,2,8192]{2,1,0:T(2,128)(2,1)S(1)} %reshape.170), channel_id=1, replica_groups=mesh['groups'=2,'seq'=16] {'seq'}, dimensions={0}, use_global_device_ids=true | all-gather | bytes 557056 | tf_op jit(solution)/shard_map/all_gather | solution.py:132
  308.7 9.5 %convolution_convert_fusion = bf16[32,1024]{1,0:T(8,128)(2,1)} fusion(bf16[32,8192]{1,0:T(8,128)(2,1)S(1)} %reshape.171, bf16[8192,1024]{1,0:T(8,128)(2,1)} %param.20), kind=kOutput, calls=%fused_computation.53 | convolution fusion | flops 536903680 | bytes 17367040 | tf_op jit(solution)/shard_map/dot_general | solution.py:133
  (74 shorter events, 5.5 us)
Async XLA Ops:
  6.5 4.6 %copy-start = (bf16[1024,512]{1,0:T(8,128)(2,1)S(1)}, bf16[1024,512]{1,0:T(8,128)(2,1)}, u32[]{:S(2)}) copy-start(bf16[1024,512]{1,0:T(8,128)(2,1)} %param.18) | copy-start | bytes 3145732
  6.5 282.1 %reduce-scatter.3.cloned.1.call-start = ((), (), s32[]{:S(2)}) async-start(), calls=%async_computation.1 | async-start | bytes 1114112 | tf_op jit(solution)/shard_map/reduce_scatter | solution.py:129
  104.8 8.0 %copy-start.2 = (s32[32]{0:T(128)S(1)}, s32[32]{0:T(128)}, u32[]{:S(2)}) copy-start(s32[32]{0:T(128)} %param.27) | copy-start | bytes 388
  104.8 8.0 %copy-start.3 = (s32[32]{0:T(128)S(1)}, s32[32]{0:T(128)}, u32[]{:S(2)}) copy-start(s32[32]{0:T(128)} %param.29) | copy-start | bytes 388
  168.6 60.8 %copy-start.4 = (u32[32]{0:T(128)S(1)}, u32[32]{0:T(128)}, u32[]{:S(2)}) copy-start(u32[32]{0:T(128)} %constant.72) | copy-start | bytes 388
  308.7 9.5 %copy-start.1 = (bf16[1024,512]{1,0:T(8,128)(2,1)S(1)}, bf16[1024,512]{1,0:T(8,128)(2,1)}, u32[]{:S(2)}) copy-start(bf16[1024,512]{1,0:T(8,128)(2,1)} %param.18) | copy-start | bytes 3145732
Sparse Core Ops, SparseCore 0:
  229.5 55.0 reduce-scatter.2
where the time goes:
time: 326 us; the launch traced here: 325 us
  blocking collectives  209 us (64%)
  matrix products  52 us (16%)
  local copies, waits for them, and re-layouts  29.1 us (9%)
  between operations  14.2 us (4%)
  other arithmetic  13.1 us (4%)
  loops' own time  7.13 us (2%)
    psum x1, blocking collectives, body(): query, s_keys, s_vals = lax.psum((part_q, part_k, part_v), 'seq')  75 us
    unnamed x1, blocking collectives  57.9 us
    pmax x1, blocking collectives, body(): peak = lax.pmax(top, 'seq')  57.6 us
    all_gather x1, blocking collectives, body(): attended = lax.all_gather(own_rows, 'seq', axis=0, tiled=True)  18.9 us
    unnamed x20, local copies, waits for them, and re-layouts  14.2 us
    dot_general x1, matrix products, body(): jnp.dot(attended, w_out, preferred_element_type=jnp.float32)  9.47 us
    reduce_sum x4, other arithmetic, head_part(): jnp.sum(e_demo, axis=1)  8.94 us
    dot_general x1, matrix products, body(): part_q = jnp.dot(hidden, w_query, preferred_element_type=jnp.float32)  8.8 us
  transfers between devices with their start and end apart: 1, of which 0 were waited for; matrix products, arithmetic and copies ran while one was open for 0% of the time, Pallas kernels for 0%

commit v1 on v0

v1 whole, which is shorter than its diff:
```python
import functools
import math

import jax
import jax.numpy as jnp
from jax import lax
from jax.experimental import pallas as pl
from jax.experimental.pallas import tpu as pltpu
from jax.sharding import PartitionSpec as P

HD = 128
NEG = -1e30
STAT = 8
F32 = jnp.float32
BF16 = jnp.bfloat16


def remote(src, dst, send, recv, dev):
    return pltpu.make_async_remote_copy(
        src_ref=src,
        dst_ref=dst,
        send_sem=send,
        recv_sem=recv,
        device_id={"seq": dev},
        device_id_type=pl.DeviceIdType.MESH,
    )


def enter(chips, chip, core):
    barrier = pltpu.get_barrier_semaphore()

    def greet(k, _):
        pl.semaphore_signal(
            barrier,
            inc=1,
            device_id={"seq": lax.rem(chip + k, chips) * 2 + core},
            device_id_type=pl.DeviceIdType.MESH,
        )
        return 0

    lax.fori_loop(1, chips, greet, 0)
    pl.semaphore_signal(
        barrier,
        inc=1,
        device_id={"seq": chip * 2 + 1 - core},
        device_id_type=pl.DeviceIdType.MESH,
    )
    pl.semaphore_wait(barrier, chips)


def gather(chips, chip, core, gat, g_send, g_recv, f_send, f_recv):
    partner = chip * 2 + 1 - core

    def to_chip(k):
        dev = lax.rem(chip + k, chips) * 2 + core
        mine = gat.at[core, chip]
        return remote(mine, gat.at[core, chip], g_send.at[k], g_recv.at[k], dev)

    def to_partner(k):
        src = lax.rem(chip - k + chips, chips)
        return remote(
            gat.at[core, src], gat.at[core, src], f_send.at[k], f_recv.at[k], partner
        )

    def from_chip(k):
        src = lax.rem(chip - k + chips, chips)
        return remote(gat.at[core, src], gat.at[core, src], g_send.at[k], g_recv.at[k], partner)

    def from_partner(k):
        src = lax.rem(chip - k + chips, chips)
        return remote(
            gat.at[1 - core, src], gat.at[1 - core, src], f_send.at[k], f_recv.at[k], partner
        )

    def start(k, _):
        to_chip(k).start()
        return 0

    lax.fori_loop(1, chips, start, 0)
    to_partner(0).start()

    def forward(k, _):
        from_chip(k).wait_recv()
        to_partner(k).start()
        return 0

    lax.fori_loop(1, chips, forward, 0)

    def arrive(k, _):
        from_partner(k).wait_recv()
        to_partner(k).wait_send()
        return 0

    lax.fori_loop(0, chips, arrive, 0)

    def drain(k, _):
        to_chip(k).wait_send()
        return 0

    lax.fori_loop(1, chips, drain, 0)


def project_kernel(
    chips, qh, kvs, hid, wq, wk, wv, out,
    wbuf, kvp, part, recv1, sums, recv2, gat,
    w_sem, s1, r1, s2, r2, g_send, g_recv, f_send, f_recv,
):
    index = lax.axis_index("seq")
    chip, core = index // 2, lax.rem(index, 2)
    partner = chip * 2 + 1 - core
    wide = qh * HD
    qt = hid.shape[0] // 2
    kvg = 2 * wk.shape[1] // HD

    def piece_of(k):
        return lax.rem(chip + 1 + k, chips)

    def load(k):
        return pltpu.make_async_copy(
            wq.at[:, pl.ds(pl.multiple_of(piece_of(k) * wide, HD), wide)],
            wbuf.at[k],
            w_sem.at[k],
        )

    def pair(k):
        return remote(part.at[1 - core, k], recv1.at[k], s1.at[k], r1.at[k], partner)

    def scatter(k):
        return remote(
            sums.at[k], recv2.at[k], s2.at[k], r2.at[k], piece_of(k) * 2 + core
        )

    def begin(k, _):
        load(k).start()
        return 0

    lax.fori_loop(0, chips, begin, 0)
    for i, w in enumerate((wk, wv)):
        res = jnp.dot(hid[...], w[...], preferred_element_type=F32)
        for g in range(kvg // 2):
            for c in range(2):
                kvp[i * (kvg // 2) + g, c] = res[c * qt : (c + 1) * qt, g * HD : (g + 1) * HD]
    enter(chips, chip, core)

    def merge(k):
        pair(k).wait_recv()
        sums[k] = part[core, k] + recv1[k]

    def step(k, _):
        load(k).wait()
        res = jnp.dot(hid[...], wbuf[k], preferred_element_type=F32)
        for c in range(2):
            for s in range(qh):
                part[c, k, s] = res[c * qt : (c + 1) * qt, s * HD : (s + 1) * HD]
            for s in range(kvs):
                part[c, k, qh + s] = kvp[lax.rem(piece_of(k) * kvs + s, kvg), c]
        pair(k).start()

        @pl.when(k > 0)
        def _():
            merge(k - 1)
            scatter(k - 1).start()

        return 0

    lax.fori_loop(0, chips, step, 0)
    merge(chips - 1)

    def collect(k, total):
        scatter(k).wait_recv()
        return total + recv2[k]

    total = lax.fori_loop(0, chips - 1, collect, sums[chips - 1])
    gat[core, chip] = total.astype(BF16)
    gather(chips, chip, core, gat, g_send, g_recv, f_send, f_recv)

    def drain(k, _):
        pair(k).wait_send()
        return 0

    lax.fori_loop(0, chips, drain, 0)

    def drain2(k, _):
        scatter(k).wait_send()
        return 0

    lax.fori_loop(0, chips - 1, drain2, 0)
    out[...] = gat[...]


def nt(a, b):
    return lax.dot_general(a, b, (((1,), (1,)), ((), ())), preferred_element_type=F32)


def tn(a, b):
    return lax.dot_general(a, b, (((0,), (0,)), ((), ())), preferred_element_type=F32)


def attend_kernel(
    qh, blk, ks, vs, q_ref, sk, sv, pk, pv, dk, dv, task_row, len_row, s_mask, out,
    s_scr, acc,
):
    h = pl.program_id(0)
    inv = 1.0 / math.sqrt(HD)
    per_head = q_ref.shape[1]
    qt = q_ref.shape[3]
    cols = qh * qt
    rows = 2 * per_head * cols
    q = jnp.concatenate(
        [q_ref[c, p, :qh].reshape(cols, HD) for c in range(2) for p in range(per_head)], axis=0
    )
    blocks = pk.shape[0] // blk
    many = math.gcd(4, blocks)
    tasks, demo_dev = dk.shape[0], dk.shape[1]
    some = math.gcd(4, tasks)

    def fold(x, op):
        return op(x.reshape(x.shape[0] // 8, 8, x.shape[1]), axis=0)

    def score(i, top):
        for b in range(many):
            at = i * many + b
            here = pl.ds(pl.multiple_of(at * blk, blk), blk)
            s = nt(pk[here, :], q) * (ks[at, h] * inv)
            s_scr[here, :] = s
            top = jnp.maximum(top, fold(s, jnp.max))
        return top

    top = lax.fori_loop(0, blocks // many, score, jnp.full((8, rows), NEG, F32))
    mine = task_row[...]

    def pick(i, best):
        for b in range(some):
            best = jnp.where(mine == i * some + b, nt(dk[i * some + b], q), best)
        return best

    s_demo = lax.fori_loop(0, tasks // some, pick, jnp.zeros((demo_dev, rows), F32))
    slot = lax.broadcasted_iota(jnp.int32, (demo_dev, rows), 0)
    s_demo = jnp.where(slot < len_row[...], s_demo * inv, NEG)
    self_k = jnp.concatenate([sk[c, 0, 0] for c in range(2)], axis=0)
    self_v = jnp.concatenate([sv[c, 0, 0] for c in range(2)], axis=0)
    s_self = jnp.where(s_mask[...] > 0, nt(self_k, q) * inv, NEG)
    top = jnp.maximum(top, jnp.maximum(fold(s_demo, jnp.max), fold(s_self, jnp.max)))
    top = jnp.max(top, axis=0, keepdims=True)

    e_demo = jnp.exp(s_demo - top)
    e_self = jnp.exp(s_self - top)
    total = fold(e_demo, jnp.sum) + fold(e_self, jnp.sum)
    acc[...] = tn(self_v, e_self.astype(BF16))

    def demo(i, _):
        weights = jnp.concatenate(
            [jnp.where(mine == i * some + b, e_demo, 0.0).astype(BF16) for b in range(some)], axis=0
        )
        here = pl.ds(i * some, some)
        acc[...] += tn(dv[here].reshape(some * demo_dev, HD), weights)
        return 0

    lax.fori_loop(0, tasks // some, demo, 0)

    def prefix(i, total):
        weights = []
        for b in range(many):
            at = i * many + b
            e = jnp.exp(s_scr[pl.ds(pl.multiple_of(at * blk, blk), blk), :] - top)
            total = total + fold(e, jnp.sum)
            weights.append((e * vs[at, h]).astype(BF16))
        here = pl.ds(pl.multiple_of(i * many * blk, blk), many * blk)
        acc[...] += tn(pv[here, :], jnp.concatenate(weights, axis=0))
        return total

    total = lax.fori_loop(0, blocks // many, prefix, total)
    total = jnp.sum(total, axis=0, keepdims=True)
    first = lax.broadcasted_iota(jnp.int32, (STAT, rows), 0) == 0
    stats = jnp.where(first, top, total)
    for c in range(2):
        for p in range(per_head):
            lanes = slice((c * per_head + p) * cols, (c * per_head + p + 1) * cols)
            out[c, p, :HD] = acc[:, lanes]
            out[c, p, HD:] = stats[:, lanes]


def output_kernel(
    chips, qh, part, wo, out,
    wbuf, recv1, sums, recv2, gat, acc,
    w_sem, s1, r1, s2, r2, g_send, g_recv, f_send, f_recv,
):
    index = lax.axis_index("seq")
    chip, core = index // 2, lax.rem(index, 2)
    partner = chip * 2 + 1 - core
    deep = qh * HD
    cols = part.shape[3]
    qt = cols // qh

    def piece_of(k):
        return lax.rem(chip + 1 + k, chips)

    def load(k):
        return pltpu.make_async_copy(
            wo.at[pl.ds(pl.multiple_of(k * deep, HD), deep), :], wbuf.at[k], w_sem.at[k]
        )

    def pair(k):
        return remote(part.at[1 - core, piece_of(k)], recv1.at[k], s1.at[k], r1.at[k], partner)

    def scatter(k):
        return remote(
            sums.at[k], recv2.at[k], s2.at[k], r2.at[k], piece_of(k) * 2 + core
        )

    enter(chips, chip, core)

    def begin(k, _):
        pair(k).start()
        return 0

    lax.fori_loop(0, chips, begin, 0)

    def begin_load(k, _):
        load(k).start()
        return 0

    lax.fori_loop(0, chips, begin_load, 0)

    def join(a, b):
        top = jnp.maximum(a[HD : HD + 1], b[HD : HD + 1])
        fa, fb = jnp.exp(a[HD : HD + 1] - top), jnp.exp(b[HD : HD + 1] - top)
        first = lax.broadcasted_iota(jnp.int32, (STAT, cols), 0) == 0
        stats = jnp.where(first, top, a[HD:] * fa + b[HD:] * fb)
        return a[:HD] * fa + b[:HD] * fb, stats

    def merge(k):
        pair(k).wait_recv()
        low, stats = join(part[core, piece_of(k)], recv1[k])
        sums[k, :HD] = low
        sums[k, HD:] = stats

    def step(k, _):
        merge(k)
        scatter(k).start()
        return 0

    lax.fori_loop(0, chips - 1, step, 0)
    merge(chips - 1)

    def arrive(k, _):
        scatter(k).wait_recv()
        return 0

    lax.fori_loop(0, chips - 1, arrive, 0)
    own = chips - 1
    top = sums[own, HD : HD + 1]
    for k in range(own):
        top = jnp.maximum(top, recv2[k, HD : HD + 1])
    factor = jnp.exp(sums[own, HD : HD + 1] - top)
    total = sums[own, HD + 1 : HD + 2] * factor
    value = sums[own, :HD] * factor
    for k in range(own):
        factor = jnp.exp(recv2[k, HD : HD + 1] - top)
        total = total + recv2[k, HD + 1 : HD + 2] * factor
        value = value + recv2[k, :HD] * factor
    rows = (value / total).T.astype(BF16)
    gat[core, chip] = rows.reshape(qh, qt, HD)
    gather(chips, chip, core, gat, g_send, g_recv, f_send, f_recv)

    def drain(k, _):
        pair(k).wait_send()
        return 0

    lax.fori_loop(0, chips, drain, 0)

    def drain2(k, _):
        scatter(k).wait_send()
        return 0

    lax.fori_loop(0, chips - 1, drain2, 0)
    acc[...] = jnp.zeros_like(acc)

    def mix(k, _):
        load(k).wait()
        left = jnp.concatenate(
            [jnp.concatenate([gat[c, k, s] for s in range(qh)], axis=1) for c in range(2)], axis=0
        )
        acc[...] += jnp.dot(left, wbuf[k], preferred_element_type=F32)
        return 0

    lax.fori_loop(0, chips, mix, 0)
    out[...] = acc[...].astype(BF16)


def sems(chips):
    return [pltpu.SemaphoreType.DMA((chips,)) for _ in range(9)]


def body(
    hidden, w_query, w_key, w_value, w_out, prefix_keys, prefix_values, key_scales, value_scales,
    demo_keys, demo_values, task_ids, demo_lengths, offsets,
):
    devices = lax.axis_size("seq")
    index = lax.axis_index("seq")
    chips = devices // 2
    qtok, depth = hidden.shape
    qt = qtok // 2
    kvh = prefix_keys.shape[1] // HD
    heads = w_query.shape[1] // HD
    group = heads // kvh
    qh = heads // chips
    kvs = max(1, 2 * kvh // chips)
    gp = qh + kvs
    cols = qh * qt
    per_head = chips // kvh
    tasks, demo_dev = demo_keys.shape[:2]
    pre_dev = prefix_keys.shape[0]
    blk = pre_dev // key_scales.shape[0]
    rows = qtok * group
    vmem = pl.BlockSpec(memory_space=pltpu.VMEM)
    hbm = pl.BlockSpec(memory_space=pl.ANY)

    query = pl.pallas_call(
        functools.partial(project_kernel, chips, qh, kvs),
        name="project",
        out_shape=jax.ShapeDtypeStruct((2, chips, gp, qt, HD), BF16),
        in_specs=[vmem, hbm, vmem, vmem],
        out_specs=vmem,
        scratch_shapes=[
            pltpu.VMEM((chips, depth, qh * HD), BF16),
            pltpu.VMEM((2 * kvh, 2, qt, HD), F32),
            pltpu.VMEM((2, chips, gp, qt, HD), F32),
            pltpu.VMEM((chips, gp, qt, HD), F32),
            pltpu.VMEM((chips, gp, qt, HD), F32),
            pltpu.VMEM((chips, gp, qt, HD), F32),
            pltpu.VMEM((2, chips, gp, qt, HD), BF16),
        ]
        + sems(chips),
        compiler_params=pltpu.CompilerParams(
            collective_id=0, has_side_effects=True, vmem_limit_bytes=48 << 20
        ),
    )(hidden, w_query, w_key, w_value)

    def by_row(x):
        return jnp.broadcast_to(x.reshape(2, 1, qt), (2, group, qt)).reshape(1, rows)

    task_row = by_row(task_ids)
    task_len = jnp.sum(
        jnp.where(task_ids[:, None] == jnp.arange(tasks)[None, :], demo_lengths[None, :], 0), axis=1
    )
    len_row = by_row(task_len - index * demo_dev)
    token = jnp.arange(qtok, dtype=jnp.int32)
    s_mask = (
        (task_ids[:, None] == task_row)
        & (offsets[:, None] <= by_row(offsets))
        & (lax.rem(token, devices) == index)[:, None]
    ).astype(jnp.int32)

    def kv_spec(first):
        return pl.BlockSpec(
            (2, 1, 1, qt, HD),
            lambda h: (0, (first + h) // kvs, qh + (first + h) % kvs, 0, 0),
        )

    def whole(shape):
        return pl.BlockSpec(shape, lambda h: (0, 0))

    smem = pl.BlockSpec(memory_space=pltpu.SMEM)
    pre_spec = pl.BlockSpec((pre_dev, HD), lambda h: (0, h))
    demo_spec = pl.BlockSpec((tasks, demo_dev, HD), lambda h: (0, 0, h))
    part = pl.pallas_call(
        functools.partial(attend_kernel, qh, blk),
        name="attend",
        grid=(kvh,),
        out_shape=jax.ShapeDtypeStruct((2, chips, HD + STAT, cols), F32),
        in_specs=[
            smem,
            smem,
            pl.BlockSpec((2, per_head, gp, qt, HD), lambda h: (0, h, 0, 0, 0)),
            kv_spec(0),
            kv_spec(kvh),
            pre_spec,
            pre_spec,
            demo_spec,
            demo_spec,
            whole((1, rows)),
            whole((1, rows)),
            whole((qtok, rows)),
        ],
        out_specs=pl.BlockSpec((2, per_head, HD + STAT, cols), lambda h: (0, h, 0, 0)),
        scratch_shapes=[pltpu.VMEM((pre_dev, rows), F32), pltpu.VMEM((HD, rows), F32)],
        compiler_params=pltpu.CompilerParams(vmem_limit_bytes=40 << 20),
    )(
        key_scales, value_scales, query, query, query, prefix_keys, prefix_values,
        demo_keys, demo_values, task_row, len_row, s_mask,
    )

    return pl.pallas_call(
        functools.partial(output_kernel, chips, qh),
        name="mix",
        out_shape=jax.ShapeDtypeStruct((qtok, w_out.shape[1]), BF16),
        in_specs=[vmem, hbm],
        out_specs=vmem,
        scratch_shapes=[
            pltpu.VMEM((chips, qh * HD, w_out.shape[1]), BF16),
            pltpu.VMEM((chips, HD + STAT, cols), F32),
            pltpu.VMEM((chips, HD + STAT, cols), F32),
            pltpu.VMEM((chips, HD + STAT, cols), F32),
            pltpu.VMEM((2, chips, qh, qt, HD), BF16),
            pltpu.VMEM((qtok, w_out.shape[1]), F32),
        ]
        + sems(chips),
        compiler_params=pltpu.CompilerParams(
            collective_id=1, has_side_effects=True, vmem_limit_bytes=48 << 20
        ),
    )(part, w_out)


def solution(mesh):
    placed = (
        P("groups", "seq"),
        P("seq", None),
        P("seq", None),
        P("seq", None),
        P(None, "seq"),
        P(("groups", "seq"), None),
        P(("groups", "seq"), None),
        P(("groups", "seq"), None),
        P(("groups", "seq"), None),
        P("groups", "seq", None),
        P("groups", "seq", None),
        P("groups"),
        P("groups"),
        P("groups"),
    )
    return jax.shard_map(
        body, mesh=mesh, in_specs=placed, out_specs=P("groups", "seq"), check_vma=False
    )
```

time: 326 us -> 99.1 us (0.30)
  blocking collectives: 209 us -> 0 us
  Pallas kernels: 0 us -> 89.8 us
  matrix products: 52 us -> 0 us
  local copies, waits for them, and re-layouts: 29.1 us -> 7.32 us
  between operations: 14.2 us -> 0.09 us
  other arithmetic: 13.1 us -> 1.53 us
  loops' own time: 7.13 us -> 0 us
    pallas_call x0 -> x3, Pallas kernels: none -> 89.8 us  [the longest x1 33.5 us: body(): pl.pallas_call(functools.partial(project_kernel, chips, qh, kvs), name='p...]
    psum x1 -> x0, blocking collectives: 75 us -> none  [body(): query, s_keys, s_vals = lax.psum((part_q, part_k, part_v), 'seq')]
    unnamed x1 -> x0, blocking collectives: 57.9 us -> none
    pmax x1 -> x0, blocking collectives: 57.6 us -> none  [body(): peak = lax.pmax(top, 'seq')]
    dot_general x28 -> x0, matrix products: 52 us -> none  [the longest x1 9.47 us: body(): jnp.dot(attended, w_out, preferred_element_type=jnp.float32)]
    all_gather x1 -> x0, blocking collectives: 18.9 us -> none  [body(): attended = lax.all_gather(own_rows, 'seq', axis=0, tiled=True)]
    reduce_sum x9 -> x1, other arithmetic: 9.8 us -> 0.76 us  [body(): jnp.sum(jnp.where(task_ids[:, None] == jnp.arange(tasks)[None, :], demo_l...]
    unnamed x20 -> x17, local copies, waits for them, and re-layouts: 14.2 us -> 5.44 us
  transfers between devices with their start and end apart: 1 -> 0, of which waited for: 0 -> 0; matrix products, arithmetic and copies ran while one was open for 0% -> 0% of each run, Pallas kernels for 0% -> 0%
where the time goes in v1:
time: 99.1 us; the launch traced here: 98.7 us
  Pallas kernels  89.8 us (91%)
  local copies, waits for them, and re-layouts  7.32 us (7%)
  other arithmetic  1.53 us (2%)
    pallas_call x1, Pallas kernels, body(): pl.pallas_call(functools.partial(project_kernel, chips, qh, kvs), name='p...  33.5 us
    pallas_call x1, Pallas kernels, body(): pl.pallas_call(functools.partial(output_kernel, chips, qh), name='mix', o...  32.6 us
    pallas_call x1, Pallas kernels, body(): pl.pallas_call(functools.partial(attend_kernel, qh, blk), name='attend',...  23.7 us
    unnamed x17, local copies, waits for them, and re-layouts  5.44 us

profile of v1, /device:TPU:0, one launch (start us, length us, event | category | flops | bytes accessed | tf_op | source)
XLA Modules:
  0.0 98.7 jit_solution(17698628853471946414)
XLA Ops:
  0.0 0.8 select_reduce_fusion
  0.8 0.1 sub.15
  0.9 0.7 broadcast_in_dim.42
  1.6 0.7 broadcast_in_dim.22
  2.3 0.8 copy.17.ks
  3.1 0.8 copy.18.vs
  3.8 0.1 eq.42
  3.9 0.1 reshape.29.task_row
  4.0 0.1 le.16
  4.1 0.1 reshape.30.len_row
  4.2 0.8 and_convert_fusion.s_mask
  4.9 0.0 copy-start.4
  5.0 1.2 %copy-done.4 = bf16[1024,512]{1,0:T(8,128)(2,1)S(1)} copy-done((bf16[1024,512]{1,0:T(8,128)(2,1)S(1)}, bf16[1024,512]{1,0:T(8,128)(2,1)}, u32[]{:S(2)}) %copy-start.4) | copy-done | bytes 1048600
  6.2 0.0 copy-start.5
  6.2 1.2 %copy-done.5 = bf16[1024,512]{1,0:T(8,128)(2,1)S(1)} copy-done((bf16[1024,512]{1,0:T(8,128)(2,1)S(1)}, bf16[1024,512]{1,0:T(8,128)(2,1)}, u32[]{:S(2)}) %copy-start.5) | copy-done | bytes 1048600
  7.4 0.0 copy-start.6
  7.4 0.8 copy-done.6
  8.2 0.0 copy-start
  8.2 0.0 copy-start.1
  8.2 0.0 copy-start.2
  8.2 0.0 copy-start.3
  8.3 33.5 %project.1.q_ref.sk.sv = bf16[2,8,9,16,128]{4,3,2,1,0:T(8,128)(2,1)S(1)} custom-call(bf16[32,1024]{1,0:T(8,128)(2,1)S(1)} %copy-done.6, bf16[1024,8192]{1,0:T(8,128)(2,1)} %wq.1, bf16[1024,512]{1,0:T(8,128)(2,1)S(1)} %copy-done.4, bf16[1024,512]{1,0:T(8,128)(2,1)S(1)} %copy-done.5), custom_call_target="tpu_custom_call" | custom-call | tf_op jit(solution)/shard_map/project/pallas_call | solution.py:419
  41.8 0.0 copy-done
  41.8 0.0 copy-done.1
  41.8 0.0 copy-done.2
  41.8 0.0 copy-done.3
  41.8 23.7 %attend.1.part = f32[2,8,136,128]{3,2,1,0:T(8,128)S(1)} custom-call(f32[16,4]{1,0:T(8,128)S(1)} %copy.17.ks, f32[16,4]{1,0:T(8,128)S(1)} %copy.18.vs, bf16[2,8,9,16,128]{4,3,2,1,0:T(8,128)(2,1)S(1)} %project.1.q_ref.sk.sv, bf16[2,8,9,16,128]{4,3,2,1,0:T(8,128)(2,1)S(1)} %project.1.q_ref.sk.sv, bf16[2,8,9,16,128]{4,3,2,1,0:T(8,128)(2,1)S(1)} %project.1.q_ref.sk.sv, ...), custom_call_target="tpu_custom_call" | custom-call | tf_op jit(solution)/shard_map/attend/pallas_call | solution.py:467
  65.5 32.6 %mix.1 = bf16[32,1024]{1,0:T(8,128)(2,1)S(1)} custom-call(f32[2,8,136,128]{3,2,1,0:T(8,128)S(1)} %attend.1.part, bf16[8192,1024]{1,0:T(8,128)(2,1)} %wo.1), custom_call_target="tpu_custom_call" | custom-call | tf_op jit(solution)/shard_map/mix/pallas_call | solution.py:494
  98.1 0.6 copy.20
  (5 shorter events, 0.0 us)
Async XLA Ops:
  4.9 1.2 %copy-start.4 = (bf16[1024,512]{1,0:T(8,128)(2,1)S(1)}, bf16[1024,512]{1,0:T(8,128)(2,1)}, u32[]{:S(2)}) copy-start(bf16[1024,512]{1,0:T(8,128)(2,1)} %wk.1) | copy-start | bytes 3145732
  6.2 1.2 %copy-start.5 = (bf16[1024,512]{1,0:T(8,128)(2,1)S(1)}, bf16[1024,512]{1,0:T(8,128)(2,1)}, u32[]{:S(2)}) copy-start(bf16[1024,512]{1,0:T(8,128)(2,1)} %wv.1) | copy-start | bytes 3145732
  7.4 0.8 copy-start.6
  8.2 33.5 %copy-start = (bf16[2048,512]{1,0:T(8,128)(2,1)S(1)}, bf16[2048,512]{1,0:T(8,128)(2,1)}, u32[]{:S(2)}) copy-start(bf16[2048,512]{1,0:T(8,128)(2,1)} %pk.1) | copy-start | bytes 6291460
  8.2 33.5 %copy-start.1 = (bf16[2048,512]{1,0:T(8,128)(2,1)S(1)}, bf16[2048,512]{1,0:T(8,128)(2,1)}, u32[]{:S(2)}) copy-start(bf16[2048,512]{1,0:T(8,128)(2,1)} %pv.1) | copy-start | bytes 6291460
  8.2 33.5 %copy-start.2 = (bf16[16,128,512]{2,1,0:T(8,128)(2,1)S(1)}, bf16[16,128,512]{2,1,0:T(8,128)(2,1)}, u32[]{:S(2)}) copy-start(bf16[16,128,512]{2,1,0:T(8,128)(2,1)} %dk.1) | copy-start | bytes 6291460
  8.2 33.5 %copy-start.3 = (bf16[16,128,512]{2,1,0:T(8,128)(2,1)S(1)}, bf16[16,128,512]{2,1,0:T(8,128)(2,1)}, u32[]{:S(2)}) copy-start(bf16[16,128,512]{2,1,0:T(8,128)(2,1)} %dv.1) | copy-start | bytes 6291460

commit v2 on v1

v2 whole, which is shorter than its diff:
```python
import functools
import math

import jax
import jax.numpy as jnp
from jax import lax
from jax.experimental import pallas as pl
from jax.experimental.pallas import tpu as pltpu
from jax.sharding import PartitionSpec as P

HD = 128
NEG = -1e30
STAT = 8
F32 = jnp.float32
BF16 = jnp.bfloat16


def remote(src, dst, send, recv, dev):
    return pltpu.make_async_remote_copy(
        src_ref=src,
        dst_ref=dst,
        send_sem=send,
        recv_sem=recv,
        device_id={"seq": dev},
        device_id_type=pl.DeviceIdType.MESH,
    )


def spot(chips, k):
    index = lax.axis_index("seq")
    chip, core = index // 2, lax.rem(index, 2)
    far, near = chip // 2, lax.rem(chip, 2)
    side = lax.rem(1 - near + lax.rem(k, 2), 2)
    return lax.rem(far + 1 + k // 2, chips // 2) * 2 + side


def enter(chips, chip, core):
    barrier = pltpu.get_barrier_semaphore()
    far, near = chip // 2, lax.rem(chip, 2)

    def hello(dev):
        pl.semaphore_signal(
            barrier, inc=1, device_id={"seq": dev}, device_id_type=pl.DeviceIdType.MESH
        )

    def greet(k, _):
        hello((lax.rem(far + k, chips // 2) * 2 + near) * 2 + core)
        return 0

    lax.fori_loop(1, chips // 2, greet, 0)
    hello((far * 2 + 1 - near) * 2 + core)
    hello(chip * 2 + 1 - core)
    pl.semaphore_wait(barrier, chips // 2 + 1)


def gather(chips, chip, core, gat, sem, use):
    z_send, z_recv, y_send, y_recv, f_send, f_recv = sem
    depth = chips // 2
    far, near = chip // 2, lax.rem(chip, 2)

    def from_far(i, side):
        return lax.rem(far - i + depth, depth) * 2 + side

    def move(c, piece, send, recv, dev):
        return remote(gat.at[c, piece], gat.at[c, piece], send, recv, dev)

    def to_far(i):
        dev = (lax.rem(far + i, depth) * 2 + near) * 2 + core
        return move(core, chip, z_send.at[i], z_recv.at[i], dev)

    def of_far(i):
        dev = (lax.rem(far + i, depth) * 2 + near) * 2 + core
        return move(core, from_far(i, near), z_send.at[i], z_recv.at[i], dev)

    def near_copy(i, side):
        dev = (far * 2 + 1 - near) * 2 + core
        return move(core, from_far(i, side), y_send.at[i], y_recv.at[i], dev)

    def core_copy(c, i, e):
        side = near if e == 0 else 1 - near
        k = 2 * i + e
        return move(c, from_far(i, side), f_send.at[k], f_recv.at[k], chip * 2 + 1 - core)

    def start(i, _):
        to_far(i).start()
        return 0

    lax.fori_loop(1, depth, start, 0)
    near_copy(0, near).start()
    core_copy(core, 0, 0).start()

    def forward(i, _):
        of_far(i).wait_recv()
        near_copy(i, near).start()
        core_copy(core, i, 0).start()
        near_copy(i - 1, 1 - near).wait_recv()
        core_copy(core, i - 1, 1).start()
        return 0

    lax.fori_loop(1, depth, forward, 0)
    near_copy(depth - 1, 1 - near).wait_recv()
    core_copy(core, depth - 1, 1).start()

    def arrive(i, _):
        for e in range(2):
            core_copy(1 - core, i, e).wait_recv()
            use(from_far(i, near if e == 0 else 1 - near))
        return 0

    lax.fori_loop(0, depth, arrive, 0)

    def drain(i, _):
        near_copy(i, near).wait_send()
        core_copy(core, i, 0).wait_send()
        core_copy(core, i, 1).wait_send()

        @pl.when(i > 0)
        def _():
            to_far(i).wait_send()

        return 0

    lax.fori_loop(0, depth, drain, 0)


def project_kernel(
    chips, qh, kvs, hid_hbm, wq, wk_hbm, wv_hbm, out,
    hid, wk, wv, wbuf, kvp, part, recv1, sums, recv_y, far_sum, recv_z, gat,
    in_sem, w_sem, s1, r1, sy, ry, sz, rz, *g_sem,
):
    index = lax.axis_index("seq")
    chip, core = index // 2, lax.rem(index, 2)
    depth = chips // 2
    far, near = chip // 2, lax.rem(chip, 2)
    wide = qh * HD
    qt = hid.shape[0] // 2
    kvg = 2 * wk.shape[1] // HD

    def load(k):
        return pltpu.make_async_copy(
            wq.at[:, pl.ds(pl.multiple_of(spot(chips, k) * wide, HD), wide)],
            wbuf.at[k],
            w_sem.at[k],
        )

    def pair(k):
        dev = chip * 2 + 1 - core
        return remote(part.at[1 - core, k], recv1.at[k], s1.at[k], r1.at[k], dev)

    def near_send(i):
        dev = (far * 2 + 1 - near) * 2 + core
        return remote(sums.at[2 * i], recv_y.at[i], sy.at[i], ry.at[i], dev)

    def far_send(i):
        dev = (lax.rem(far + 1 + i, depth) * 2 + near) * 2 + core
        return remote(far_sum.at[i], recv_z.at[i], sz.at[i], rz.at[i], dev)

    small = [
        pltpu.make_async_copy(src, dst, in_sem.at[i])
        for i, (src, dst) in enumerate(((hid_hbm, hid), (wk_hbm, wk), (wv_hbm, wv)))
    ]
    for copy in small:
        copy.start()

    def begin(k, _):
        load(k).start()
        return 0

    lax.fori_loop(0, chips, begin, 0)
    enter(chips, chip, core)
    for copy in small:
        copy.wait()
    for i, w in enumerate((wk, wv)):
        res = jnp.dot(hid[...], w[...], preferred_element_type=F32)
        for g in range(kvg // 2):
            for c in range(2):
                kvp[i * (kvg // 2) + g, c] = res[c * qt : (c + 1) * qt, g * HD : (g + 1) * HD]

    def step(i, _):
        @pl.when(i < depth)
        def _():
            for e in range(2):
                k = 2 * i + e
                load(k).wait()
                res = jnp.dot(hid[...], wbuf[k], preferred_element_type=F32)
                for c in range(2):
                    for s in range(qh):
                        part[c, k, s] = res[c * qt : (c + 1) * qt, s * HD : (s + 1) * HD]
                    for s in range(kvs):
                        part[c, k, qh + s] = kvp[lax.rem(spot(chips, k) * kvs + s, kvg), c]
                pair(k).start()

        @pl.when((i > 0) & (i <= depth))
        def _():
            for e in range(2):
                k = 2 * (i - 1) + e
                pair(k).wait_recv()
                sums[k] = part[core, k] + recv1[k]
                if e == 0:
                    near_send(i - 1).start()

        @pl.when(i > 1)
        def _():
            j = i - 2
            near_send(j).wait_recv()
            far_sum[j] = sums[2 * j + 1] + recv_y[j]

            @pl.when(j < depth - 1)
            def _():
                far_send(j).start()

        return 0

    lax.fori_loop(0, depth + 2, step, 0)

    def collect(i, total):
        far_send(i).wait_recv()
        return total + recv_z[i]

    total = lax.fori_loop(0, depth - 1, collect, far_sum[depth - 1])
    gat[core, chip] = total.astype(BF16)
    gather(chips, chip, core, gat, g_sem, lambda piece: None)

    def drain(i, _):
        pair(2 * i).wait_send()
        pair(2 * i + 1).wait_send()
        near_send(i).wait_send()

        @pl.when(i < depth - 1)
        def _():
            far_send(i).wait_send()

        return 0

    lax.fori_loop(0, depth, drain, 0)
    out[...] = gat[...]


def nt(a, b):
    return lax.dot_general(a, b, (((1,), (1,)), ((), ())), preferred_element_type=F32)


def tn(a, b):
    return lax.dot_general(a, b, (((0,), (0,)), ((), ())), preferred_element_type=F32)


def attend_kernel(
    devices, qh, blk, ks, vs, tasks_of, lens, offs, q_ref, sk, sv, pk, pv, dk, dv, out,
    s_scr, acc, task_row, len_row, s_mask,
):
    h = pl.program_id(0)
    inv = 1.0 / math.sqrt(HD)
    per_head = q_ref.shape[1]
    qt = q_ref.shape[3]
    cols = qh * qt
    rows = 2 * per_head * cols
    q = jnp.concatenate(
        [q_ref[c, p, :qh].reshape(cols, HD) for c in range(2) for p in range(per_head)], axis=0
    )
    blocks = pk.shape[0] // blk
    many = math.gcd(4, blocks)
    tasks, demo_dev = dk.shape[0], dk.shape[1]
    some = math.gcd(4, tasks)

    @pl.when(h == 0)
    def _():
        index = lax.axis_index("seq")
        lane = lax.broadcasted_iota(jnp.int32, (1, rows), 1)
        token = (lane // (rows // 2)) * qt + lax.rem(lane, qt)
        zero = jnp.zeros((1, rows), jnp.int32)

        def spread(t, carry):
            task = tasks_of[t]
            here = token == t
            left = lens[task] - index * demo_dev
            values = (task, left, offs[t])
            return tuple(jnp.where(here, v, old) for v, old in zip(values, carry))

        task_all, len_all, off_all = lax.fori_loop(0, 2 * qt, spread, (zero, zero, zero))
        task_row[...] = task_all
        len_row[...] = len_all

        def allow(u, _):
            mine = jnp.where(lax.rem(u, devices) == index, tasks_of[u], -1)
            keep = (task_all == mine) & (off_all >= offs[u])
            s_mask[pl.ds(u, 1), :] = keep.astype(jnp.int32)
            return 0

        lax.fori_loop(0, 2 * qt, allow, 0)

    def fold(x, op):
        return op(x.reshape(x.shape[0] // 8, 8, x.shape[1]), axis=0)

    def score(i, top):
        for b in range(many):
            at = i * many + b
            here = pl.ds(pl.multiple_of(at * blk, blk), blk)
            s = nt(pk[here, :], q) * (ks[h, at] * inv)
            s_scr[here, :] = s
            top = jnp.maximum(top, fold(s, jnp.max))
        return top

    top = lax.fori_loop(0, blocks // many, score, jnp.full((8, rows), NEG, F32))
    mine = task_row[...]

    def pick(i, best):
        for b in range(some):
            best = jnp.where(mine == i * some + b, nt(dk[i * some + b], q), best)
        return best

    s_demo = lax.fori_loop(0, tasks // some, pick, jnp.zeros((demo_dev, rows), F32))
    slot = lax.broadcasted_iota(jnp.int32, (demo_dev, rows), 0)
    s_demo = jnp.where(slot < len_row[...], s_demo * inv, NEG)
    self_k = jnp.concatenate([sk[c, 0, 0] for c in range(2)], axis=0)
    self_v = jnp.concatenate([sv[c, 0, 0] for c in range(2)], axis=0)
    s_self = jnp.where(s_mask[...] > 0, nt(self_k, q) * inv, NEG)
    top = jnp.maximum(top, jnp.maximum(fold(s_demo, jnp.max), fold(s_self, jnp.max)))
    top = jnp.max(top, axis=0, keepdims=True)

    e_demo = jnp.exp(s_demo - top)
    e_self = jnp.exp(s_self - top)
    total = fold(e_demo, jnp.sum) + fold(e_self, jnp.sum)
    acc[...] = tn(self_v, e_self.astype(BF16))

    def demo(i, _):
        weights = jnp.concatenate(
            [jnp.where(mine == i * some + b, e_demo, 0.0).astype(BF16) for b in range(some)], axis=0
        )
        here = pl.ds(i * some, some)
        acc[...] += tn(dv[here].reshape(some * demo_dev, HD), weights)
        return 0

    lax.fori_loop(0, tasks // some, demo, 0)

    def prefix(i, total):
        weights = []
        for b in range(many):
            at = i * many + b
            e = jnp.exp(s_scr[pl.ds(pl.multiple_of(at * blk, blk), blk), :] - top)
            total = total + fold(e, jnp.sum)
            weights.append((e * vs[h, at]).astype(BF16))
        here = pl.ds(pl.multiple_of(i * many * blk, blk), many * blk)
        acc[...] += tn(pv[here, :], jnp.concatenate(weights, axis=0))
        return total

    total = lax.fori_loop(0, blocks // many, prefix, total)
    total = jnp.sum(total, axis=0, keepdims=True)
    first = lax.broadcasted_iota(jnp.int32, (STAT, rows), 0) == 0
    stats = jnp.where(first, top, total)
    for c in range(2):
        for p in range(per_head):
            lanes = slice((c * per_head + p) * cols, (c * per_head + p + 1) * cols)
            out[c, p, :HD] = acc[:, lanes]
            out[c, p, HD:] = stats[:, lanes]


def output_kernel(
    chips, qh, part, wo, out,
    wbuf, recv1, keep, y_val, y_stat, yr_val, yr_stat, z_val, z_stat, zr_val, zr_stat, gat, acc,
    w_sem, s1, r1, sy, ry, sz, rz, sy2, ry2, sz2, rz2, *g_sem,
):
    index = lax.axis_index("seq")
    chip, core = index // 2, lax.rem(index, 2)
    depth = chips // 2
    far, near = chip // 2, lax.rem(chip, 2)
    deep = qh * HD
    cols = part.shape[3]
    qt = cols // qh

    def load(k):
        return pltpu.make_async_copy(
            wo.at[pl.ds(pl.multiple_of(k * deep, HD), deep), :], wbuf.at[k], w_sem.at[k]
        )

    def pair(k):
        dev = chip * 2 + 1 - core
        src = part.at[1 - core, spot(chips, k)]
        return remote(src, recv1.at[k], s1.at[k], r1.at[k], dev)

    def near_send(i):
        dev = (far * 2 + 1 - near) * 2 + core
        return (
            remote(y_stat.at[i], yr_stat.at[i], sy2.at[i], ry2.at[i], dev),
            remote(y_val.at[i], yr_val.at[i], sy.at[i], ry.at[i], dev),
        )

    def far_send(i):
        dev = (lax.rem(far + 1 + i, depth) * 2 + near) * 2 + core
        return (
            remote(z_stat.at[i], zr_stat.at[i], sz2.at[i], rz2.at[i], dev),
            remote(z_val.at[i], zr_val.at[i], sz.at[i], rz.at[i], dev),
        )

    enter(chips, chip, core)

    def begin(k, _):
        pair(k).start()
        return 0

    lax.fori_loop(0, chips, begin, 0)

    def begin_load(k, _):
        load(k).start()
        return 0

    lax.fori_loop(0, chips, begin_load, 0)
    first = lax.broadcasted_iota(jnp.int32, (STAT, cols), 0) == 0

    def join(a, a_stat, b, b_stat):
        top = jnp.maximum(a_stat[:1], b_stat[:1])
        fa, fb = jnp.exp(a_stat[:1] - top), jnp.exp(b_stat[:1] - top)
        stat = jnp.where(first, top, a_stat * fa + b_stat * fb)
        return a.astype(F32) * fa + b.astype(F32) * fb, stat

    def merge(k):
        pair(k).wait_recv()
        at = spot(chips, k)
        return join(part[core, at, :HD], part[core, at, HD:], recv1[k, :HD], recv1[k, HD:])

    def step(i, _):
        @pl.when(i < depth)
        def _():
            value, stat = merge(2 * i)
            y_val[i] = value.astype(BF16)
            y_stat[i] = stat
            for copy in near_send(i):
                copy.start()
            value, stat = merge(2 * i + 1)
            keep[i, :HD] = value
            keep[i, HD:] = stat

        @pl.when(i > 0)
        def _():
            j = i - 1
            for copy in near_send(j):
                copy.wait_recv()
            value, stat = join(keep[j, :HD], keep[j, HD:], yr_val[j], yr_stat[j])

            @pl.when(j < depth - 1)
            def _():
                z_val[j] = value.astype(BF16)
                z_stat[j] = stat
                for copy in far_send(j):
                    copy.start()

            @pl.when(j == depth - 1)
            def _():
                keep[j, :HD] = value
                keep[j, HD:] = stat

        return 0

    lax.fori_loop(0, depth + 1, step, 0)

    def arrive(i, _):
        for copy in far_send(i):
            copy.wait_recv()
        return 0

    lax.fori_loop(0, depth - 1, arrive, 0)
    own = depth - 1
    top = keep[own, HD : HD + 1]
    for k in range(own):
        top = jnp.maximum(top, zr_stat[k, :1])
    factor = jnp.exp(keep[own, HD : HD + 1] - top)
    total = keep[own, HD + 1 : HD + 2] * factor
    value = keep[own, :HD] * factor
    for k in range(own):
        factor = jnp.exp(zr_stat[k, :1] - top)
        total = total + zr_stat[k, 1:2] * factor
        value = value + zr_val[k].astype(F32) * factor
    rows = (value / total).T.astype(BF16)
    gat[core, chip] = rows.reshape(qh, qt, HD)
    acc[...] = jnp.zeros_like(acc)

    def mix(piece):
        load(piece).wait()
        left = jnp.concatenate(
            [
                jnp.concatenate([gat[c, piece, s] for s in range(qh)], axis=1)
                for c in range(2)
            ],
            axis=0,
        )
        acc[...] += jnp.dot(left, wbuf[piece], preferred_element_type=F32)

    gather(chips, chip, core, gat, g_sem, mix)

    def drain(i, _):
        pair(2 * i).wait_send()
        pair(2 * i + 1).wait_send()
        for copy in near_send(i):
            copy.wait_send()

        @pl.when(i < depth - 1)
        def _():
            for copy in far_send(i):
                copy.wait_send()

        return 0

    lax.fori_loop(0, depth, drain, 0)
    out[...] = acc[...].astype(BF16)


def sems(*counts):
    return [pltpu.SemaphoreType.DMA((n,)) for n in counts]


def body(
    hidden, w_query, w_key, w_value, w_out, prefix_keys, prefix_values, key_scales, value_scales,
    demo_keys, demo_values, task_ids, demo_lengths, offsets,
):
    devices = lax.axis_size("seq")
    chips = devices // 2
    half = chips // 2
    qtok, depth = hidden.shape
    qt = qtok // 2
    kvh = prefix_keys.shape[1] // HD
    heads = w_query.shape[1] // HD
    group = heads // kvh
    qh = heads // chips
    kvs = max(1, 2 * kvh // chips)
    gp = qh + kvs
    cols = qh * qt
    per_head = chips // kvh
    tasks, demo_dev = demo_keys.shape[:2]
    pre_dev = prefix_keys.shape[0]
    blk = pre_dev // key_scales.shape[0]
    rows = qtok * group
    vmem = pl.BlockSpec(memory_space=pltpu.VMEM)
    hbm = pl.BlockSpec(memory_space=pltpu.HBM)

    query = pl.pallas_call(
        functools.partial(project_kernel, chips, qh, kvs),
        name="project",
        out_shape=jax.ShapeDtypeStruct((2, chips, gp, qt, HD), BF16),
        in_specs=[hbm, hbm, hbm, hbm],
        out_specs=vmem,
        scratch_shapes=[
            pltpu.VMEM(hidden.shape, BF16),
            pltpu.VMEM(w_key.shape, BF16),
            pltpu.VMEM(w_value.shape, BF16),
            pltpu.VMEM((chips, depth, qh * HD), BF16),
            pltpu.VMEM((2 * kvh, 2, qt, HD), F32),
            pltpu.VMEM((2, chips, gp, qt, HD), F32),
            pltpu.VMEM((chips, gp, qt, HD), F32),
            pltpu.VMEM((chips, gp, qt, HD), F32),
            pltpu.VMEM((half, gp, qt, HD), F32),
            pltpu.VMEM((half, gp, qt, HD), F32),
            pltpu.VMEM((half, gp, qt, HD), F32),
            pltpu.VMEM((2, chips, gp, qt, HD), BF16),
        ]
        + sems(3, chips, chips, chips, *[half] * 8, chips, chips),
        compiler_params=pltpu.CompilerParams(
            collective_id=0, has_side_effects=True, vmem_limit_bytes=48 << 20
        ),
    )(hidden, w_query, w_key, w_value)

    def kv_spec(first):
        return pl.BlockSpec(
            (2, 1, 1, qt, HD),
            lambda h: (0, (first + h) // kvs, qh + (first + h) % kvs, 0, 0),
        )

    smem = pl.BlockSpec(memory_space=pltpu.SMEM)
    pre_spec = pl.BlockSpec((pre_dev, HD), lambda h: (0, h))
    demo_spec = pl.BlockSpec((tasks, demo_dev, HD), lambda h: (0, 0, h))
    part = pl.pallas_call(
        functools.partial(attend_kernel, devices, qh, blk),
        name="attend",
        grid=(kvh,),
        out_shape=jax.ShapeDtypeStruct((2, chips, HD + STAT, cols), F32),
        in_specs=[
            *[smem] * 5,
            pl.BlockSpec((2, per_head, gp, qt, HD), lambda h: (0, h, 0, 0, 0)),
            kv_spec(0),
            kv_spec(kvh),
            pre_spec,
            pre_spec,
            demo_spec,
            demo_spec,
        ],
        out_specs=pl.BlockSpec((2, per_head, HD + STAT, cols), lambda h: (0, h, 0, 0)),
        scratch_shapes=[
            pltpu.VMEM((pre_dev, rows), F32),
            pltpu.VMEM((HD, rows), F32),
            pltpu.VMEM((1, rows), jnp.int32),
            pltpu.VMEM((1, rows), jnp.int32),
            pltpu.VMEM((qtok, rows), jnp.int32),
        ],
        compiler_params=pltpu.CompilerParams(vmem_limit_bytes=40 << 20),
    )(
        key_scales.T, value_scales.T, task_ids, demo_lengths, offsets, query, query, query,
        prefix_keys, prefix_values, demo_keys, demo_values,
    )

    return pl.pallas_call(
        functools.partial(output_kernel, chips, qh),
        name="mix",
        out_shape=jax.ShapeDtypeStruct((qtok, w_out.shape[1]), BF16),
        in_specs=[vmem, hbm],
        out_specs=vmem,
        scratch_shapes=[
            pltpu.VMEM((chips, qh * HD, w_out.shape[1]), BF16),
            pltpu.VMEM((chips, HD + STAT, cols), F32),
            pltpu.VMEM((half, HD + STAT, cols), F32),
            *[
                pltpu.VMEM((half, extent, cols), kind)
                for _ in range(4)
                for extent, kind in ((HD, BF16), (STAT, F32))
            ],
            pltpu.VMEM((2, chips, qh, qt, HD), BF16),
            pltpu.VMEM((qtok, w_out.shape[1]), F32),
        ]
        + sems(chips, chips, chips, *[half] * 12, chips, chips),
        compiler_params=pltpu.CompilerParams(
            collective_id=1, has_side_effects=True, vmem_limit_bytes=48 << 20
        ),
    )(part, w_out)


def solution(mesh):
    placed = (
        P("groups", "seq"),
        P("seq", None),
        P("seq", None),
        P("seq", None),
        P(None, "seq"),
        P(("groups", "seq"), None),
        P(("groups", "seq"), None),
        P(("groups", "seq"), None),
        P(("groups", "seq"), None),
        P("groups", "seq", None),
        P("groups", "seq", None),
        P("groups"),
        P("groups"),
        P("groups"),
    )
    return jax.shard_map(
        body, mesh=mesh, in_specs=placed, out_specs=P("groups", "seq"), check_vma=False
    )
```

time: 99.1 us -> 88.4 us (0.89)
  Pallas kernels: 89.8 us -> 84.1 us
  local copies, waits for them, and re-layouts: 7.32 us -> 3.96 us
  other arithmetic: 1.53 us -> 0 us
    pallas_call x1, Pallas kernels: 32.6 us -> 26.9 us  [body(): pl.pallas_call(functools.partial(output_kernel, chips, qh), name='mix', o...]
    unnamed x17 -> x25, local copies, waits for them, and re-layouts: 5.44 us -> 3.96 us
    broadcast_in_dim x5 -> x0, local copies, waits for them, and re-layouts: 1.48 us -> none  [by_row(): jnp.broadcast_to(x.reshape(2, 1, qt), (2, group, qt)).reshape(1, rows)]
where the time goes in v2:
time: 88.4 us; the launch traced here: 88.2 us
  Pallas kernels  84.1 us (95%)
  local copies, waits for them, and re-layouts  3.96 us (4%)
    pallas_call x1, Pallas kernels, body(): pl.pallas_call(functools.partial(project_kernel, chips, qh, kvs), name='p...  32.8 us
    pallas_call x1, Pallas kernels, body(): pl.pallas_call(functools.partial(output_kernel, chips, qh), name='mix', o...  26.9 us
    pallas_call x1, Pallas kernels, body(): pl.pallas_call(functools.partial(attend_kernel, devices, qh, blk), name='...  24.4 us
    unnamed x25, local copies, waits for them, and re-layouts  3.96 us

profile of v2, /device:TPU:0, one launch (start us, length us, event | category | flops | bytes accessed | tf_op | source)
XLA Modules:
  0.0 88.2 jit_solution(1681441171785263536)
XLA Ops:
  0.0 0.0 copy-start.4
  0.0 1.2 %copy-done.4 = bf16[1024,512]{1,0:T(8,128)(2,1)S(1)} copy-done((bf16[1024,512]{1,0:T(8,128)(2,1)S(1)}, bf16[1024,512]{1,0:T(8,128)(2,1)}, u32[]{:S(2)}) %copy-start.4) | copy-done | bytes 1048600
  1.2 0.0 copy-start.5
  1.2 1.2 %copy-done.5 = bf16[1024,512]{1,0:T(8,128)(2,1)S(1)} copy-done((bf16[1024,512]{1,0:T(8,128)(2,1)S(1)}, bf16[1024,512]{1,0:T(8,128)(2,1)}, u32[]{:S(2)}) %copy-start.5) | copy-done | bytes 1048600
  2.5 0.0 copy-start.6
  2.5 0.8 copy-done.6
  3.3 0.0 copy-start
  3.3 0.0 copy-start.1
  3.3 0.0 copy-start.2
  3.3 0.0 copy-start.3
  3.3 0.0 copy-start.7
  3.3 0.0 copy-start.8
  3.3 0.0 copy-start.9
  3.3 0.0 copy-start.10
  3.3 0.0 copy-start.11
  3.4 32.8 %project.1.q_ref.sk.sv = bf16[2,8,9,16,128]{4,3,2,1,0:T(8,128)(2,1)S(1)} custom-call(bf16[32,1024]{1,0:T(8,128)(2,1)S(1)} %copy-done.6, bf16[1024,8192]{1,0:T(8,128)(2,1)} %wq.1, bf16[1024,512]{1,0:T(8,128)(2,1)S(1)} %copy-done.4, bf16[1024,512]{1,0:T(8,128)(2,1)S(1)} %copy-done.5), custom_call_target="tpu_custom_call" | custom-call | tf_op jit(solution)/shard_map/project/pallas_call | solution.py:534
  36.2 0.0 copy-done
  36.2 0.0 copy-done.1
  36.2 0.0 copy-done.2
  36.2 0.0 copy-done.3
  36.2 0.0 copy-done.7
  36.2 0.0 copy-done.8
  36.2 0.0 copy-done.9
  36.2 0.0 copy-done.10
  36.2 0.0 copy-done.11
  36.3 24.4 %attend.1.part = f32[2,8,136,128]{3,2,1,0:T(8,128)S(1)} custom-call(f32[4,16]{1,0:T(4,128)S(1)} %bitcast.2, f32[4,16]{1,0:T(4,128)S(1)} %bitcast.3, s32[32]{0:T(128)S(1)} %copy-done.9, s32[16]{0:T(128)S(1)} %copy-done.10, s32[32]{0:T(128)S(1)} %copy-done.11, bf16[2,8,9,16,128]{4,3,2,1,0:T(8,128)(2,1)S(1)} %project.1.q_ref.sk.sv, ...), custom_call_target="tpu_custom_call" | custom-call | tf_op jit(solution)/shard_map/attend/pallas_call | solution.py:569
  60.6 26.9 %mix.1 = bf16[32,1024]{1,0:T(8,128)(2,1)S(1)} custom-call(f32[2,8,136,128]{3,2,1,0:T(8,128)S(1)} %attend.1.part, bf16[8192,1024]{1,0:T(8,128)(2,1)} %wo.1), custom_call_target="tpu_custom_call" | custom-call | tf_op jit(solution)/shard_map/mix/pallas_call | solution.py:598
  87.5 0.6 copy.16
Async XLA Ops:
  0.0 1.2 %copy-start.4 = (bf16[1024,512]{1,0:T(8,128)(2,1)S(1)}, bf16[1024,512]{1,0:T(8,128)(2,1)}, u32[]{:S(2)}) copy-start(bf16[1024,512]{1,0:T(8,128)(2,1)} %wk_hbm.1) | copy-start | bytes 3145732
  1.2 1.2 %copy-start.5 = (bf16[1024,512]{1,0:T(8,128)(2,1)S(1)}, bf16[1024,512]{1,0:T(8,128)(2,1)}, u32[]{:S(2)}) copy-start(bf16[1024,512]{1,0:T(8,128)(2,1)} %wv_hbm.1) | copy-start | bytes 3145732
  2.5 0.8 copy-start.6
  3.3 32.9 %copy-start = (bf16[2048,512]{1,0:T(8,128)(2,1)S(1)}, bf16[2048,512]{1,0:T(8,128)(2,1)}, u32[]{:S(2)}) copy-start(bf16[2048,512]{1,0:T(8,128)(2,1)} %pk.1) | copy-start | bytes 6291460
  3.3 32.9 %copy-start.1 = (bf16[2048,512]{1,0:T(8,128)(2,1)S(1)}, bf16[2048,512]{1,0:T(8,128)(2,1)}, u32[]{:S(2)}) copy-start(bf16[2048,512]{1,0:T(8,128)(2,1)} %pv.1) | copy-start | bytes 6291460
  3.3 32.9 %copy-start.2 = (bf16[16,128,512]{2,1,0:T(8,128)(2,1)S(1)}, bf16[16,128,512]{2,1,0:T(8,128)(2,1)}, u32[]{:S(2)}) copy-start(bf16[16,128,512]{2,1,0:T(8,128)(2,1)} %dk.1) | copy-start | bytes 6291460
  3.3 32.9 %copy-start.3 = (bf16[16,128,512]{2,1,0:T(8,128)(2,1)S(1)}, bf16[16,128,512]{2,1,0:T(8,128)(2,1)}, u32[]{:S(2)}) copy-start(bf16[16,128,512]{2,1,0:T(8,128)(2,1)} %dv.1) | copy-start | bytes 6291460
  3.3 32.9 %copy-start.7 = (f32[16,4]{0,1:T(4,128)S(1)}, f32[16,4]{0,1:T(4,128)}, u32[]{:S(2)}) copy-start(f32[16,4]{0,1:T(4,128)} %param.21) | copy-start | bytes 772
  3.3 32.9 %copy-start.8 = (f32[16,4]{0,1:T(4,128)S(1)}, f32[16,4]{0,1:T(4,128)}, u32[]{:S(2)}) copy-start(f32[16,4]{0,1:T(4,128)} %param.22) | copy-start | bytes 772
  3.3 32.9 %copy-start.9 = (s32[32]{0:T(128)S(1)}, s32[32]{0:T(128)}, u32[]{:S(2)}) copy-start(s32[32]{0:T(128)} %tasks_of.1) | copy-start | bytes 388
  3.3 32.9 %copy-start.10 = (s32[16]{0:T(128)S(1)}, s32[16]{0:T(128)}, u32[]{:S(2)}) copy-start(s32[16]{0:T(128)} %lens.1) | copy-start | bytes 196
  3.3 32.9 %copy-start.11 = (s32[32]{0:T(128)S(1)}, s32[32]{0:T(128)}, u32[]{:S(2)}) copy-start(s32[32]{0:T(128)} %offs.1) | copy-start | bytes 388
